TPU v7x, 512 devices: a whole 4x4x16 slice. The times are simulated.
512 devices in a mesh: level: 16 (over z_hi, y, core), dom: 32 (over z_lo, x).
Axes of the slice: x: 4, y: 4, z: 16 (z_hi: 2, z_lo: 8; z = z_hi * 8 + z_lo), core: 2. Of those that a mesh axis runs over, the one named last changes fastest.
Arguments:
- right_side: float32 [128, 256, 128], P('dom', 'level'), may hold values from -6 to 6
- fine_blocks: float32 [128, 8, 128, 128], P('dom'), may hold values from -0.06 to 0.06
- fine_cols: int32 [128, 8], P('dom'), may hold values from 0 to 7, as said below
- fine_edges: int32 [64], P('dom'), may hold values from 0 to 3, as said below
- mid_blocks: float32 [64, 8, 128, 128], P('dom'), may hold values from -0.06 to 0.06
- mid_cols: int32 [64, 8], P('dom'), may hold values from 0 to 3, as said below
- mid_edges: int32 [32], P('dom'), may hold values from 0 to 1, as said below
- fine_map: int32 [128], P('dom'), may hold values from 0 to 1, as said below
- mid_map: int32 [64], P('dom'), may hold values from 0 to 7, as said below
- coarse_inverse: float32 [1024, 1024], P('level'), may hold values from -0.1875 to 0.1875
Outputs:
- solution: float32 [128, 256, 128], P('dom', 'level')
Inputs may be any that keep to these rules, and one draw needn't show every extreme that they name: `fine_cols`: slot 0 of every block row is the row itself; each row refers to a boundary row of its lower and of its upper partition where these exist, and never past the first or last partition; slots may repeat. `fine_edges`: distinct within each partition. `mid_cols`: slot 0 of every block row is the row itself; each row refers to a boundary row of its lower and of its upper partition where these exist, and never past the first or last partition; slots may repeat. `mid_edges`: distinct within each partition. `fine_map`: each middle block row of a partition receives exactly two of its fine block rows. `mid_map`: each coarse block row receives exactly 8 middle block rows, from any partitions.
All inputs are finite; a program needn't handle non-finite values.
Results may differ from a plain program's by a relative error of at most 0.0003.
Values sent between devices are 32-bit elements; how exact they have to be, the bound alone decides.
A program may use at most 64 MiB of HBM per device.

v0:
```python
import jax
import jax.numpy as jnp
from jax import lax
from jax.sharding import PartitionSpec as P

CAGG = 8
DEG = 4


CENTRE = 1.0
HALF_WIDTH = 0.7
DAMPING = 0.7
MID_WEIGHT = 0.5**0.5


def padded(block, sides, width):
    for axis, dim in sides:
        count = lax.axis_size(axis)
        forward = [(i, i + 1) for i in range(count - 1)]
        backward = [(target, source) for source, target in forward]
        low = lax.ppermute(
            lax.slice_in_dim(block, block.shape[dim] - width, None, axis=dim), axis, forward
        )
        high = lax.ppermute(lax.slice_in_dim(block, 0, width, axis=dim), axis, backward)
        block = jnp.concatenate([low, block, high], axis=dim)
    return block


def boundary_apply(blocks, col_local, edge_list, values):
    margin = edge_list.shape[0]
    edge_rows = jnp.take(values, edge_list, axis=0)
    bordered = padded(edge_rows, (("dom", 0),), margin)
    extended = jnp.concatenate([values, bordered[:margin], bordered[2 * margin :]], axis=0)
    picked = jnp.take(extended, col_local, axis=0)
    return values + jnp.einsum("rkab,rkvb->rva", blocks, picked, precision=lax.Precision.HIGHEST)


def smooth(apply_fn, source):
    sigma_ratio = CENTRE / HALF_WIDTH
    rho_prev = 1.0 / sigma_ratio
    step_dir = source / CENTRE
    result = step_dir
    for sweep_index in range(DEG - 1):
        rho_next = 1.0 / (2.0 * sigma_ratio - rho_prev)
        step_dir = rho_next * rho_prev * step_dir + 2.0 * rho_next / HALF_WIDTH * (
            source - apply_fn(result)
        )
        result = result + step_dir
        rho_prev = rho_next
    return result


def shards(
    right_side,
    fine_blocks,
    fine_cols,
    fine_edges,
    mid_blocks,
    mid_cols,
    mid_edges,
    fine_map,
    mid_map,
    coarse_inverse,
):
    mid_rows = mid_blocks.shape[0]
    rhs_count = right_side.shape[1]
    block_order = right_side.shape[2]
    coarse_rows = coarse_inverse.shape[1] // block_order
    coarse_weight = CAGG ** (-0.5)
    fine_join = (fine_map[None, :] == jnp.arange(mid_rows, dtype=jnp.int32)[:, None]).astype(
        jnp.float32
    )
    coarse_join = (mid_map[None, :] == jnp.arange(coarse_rows, dtype=jnp.int32)[:, None]).astype(
        jnp.float32
    )

    def fine_apply(values):
        return boundary_apply(fine_blocks, fine_cols, fine_edges, values)

    def mid_apply(values):
        return boundary_apply(mid_blocks, mid_cols, mid_edges, values)

    full_inverse = lax.all_gather(coarse_inverse, "level", axis=0, tiled=True).reshape(
        coarse_rows * block_order, coarse_rows, block_order
    )
    fine_corr = smooth(fine_apply, right_side)
    mid_res = MID_WEIGHT * jnp.einsum(
        "mr,rvb->mvb", fine_join, right_side, precision=lax.Precision.HIGHEST
    )
    mid_corr = smooth(mid_apply, mid_res)
    coarse_part = jnp.einsum("cm,mvb->cvb", coarse_join, mid_res, precision=lax.Precision.HIGHEST)
    coarse_res = coarse_weight * lax.psum(coarse_part, "dom")
    coarse_flat = jnp.einsum(
        "ocb,cvb->vo", full_inverse, coarse_res, precision=lax.Precision.HIGHEST
    )
    coarse_corr = coarse_flat.reshape(rhs_count, coarse_rows, block_order).transpose(1, 0, 2)
    joined = mid_corr + coarse_weight * jnp.einsum(
        "cm,cvb->mvb", coarse_join, coarse_corr, precision=lax.Precision.HIGHEST
    )
    spread = jnp.einsum("mr,mvb->rvb", fine_join, joined, precision=lax.Precision.HIGHEST)
    solution = DAMPING * (fine_corr + MID_WEIGHT * spread)
    return solution


def solution(mesh):
    in_specs = (
        P("dom", "level", None),
        P("dom", None, None, None),
        P("dom", None),
        P("dom"),
        P("dom", None, None, None),
        P("dom", None),
        P("dom"),
        P("dom"),
        P("dom"),
        P("level", None),
    )
    out_specs = P("dom", "level", None)
    return jax.shard_map(shards, mesh=mesh, in_specs=in_specs, out_specs=out_specs, check_vma=False)
```

profile of v0, /device:TPU:8, one launch (start us, length us, event | category | flops | bytes accessed | tf_op | source)
XLA Modules:
  0.0 505.5 jit_solution(6056695034072690597)
XLA Ops:
  7.4 0.7 all-gather.2.cloned.1.call-update
  8.1 0.7 compare_select_fusion.2
  8.9 1.3 gather_fusion
  10.2 0.7 compare_and_fusion.2
  10.9 1.3 collective-permute-start.1
  12.2 4.5 collective-permute-start
  17.5 0.9 broadcast_multiply_fusion
  18.4 1.3 collective-permute-start.7
  19.7 4.5 collective-permute-start.6
  24.3 0.8 fusion.55
  25.1 0.6 copy.30
  25.8 0.7 compare_and_fusion
  26.5 0.7 compare_select_fusion.1
  27.1 1.3 compare_and_fusion.1
  28.4 0.7 compare_select_fusion
  29.3 0.6 gather_fusion.6
  29.9 2.2 convolution_bitcast_fusion.4
  32.2 1.3 collective-permute-start.9
  33.5 4.5 collective-permute-start.8
  38.0 0.6 pad_clamp_fusion.1
  38.6 0.8 collective-permute-done.8
  39.4 0.6 gather_fusion.7
  40.0 1.0 convolution_bitcast_fusion.3
  41.0 0.7 fusion.72
  41.6 0.6 broadcast_select_fusion
  42.2 1.3 collective-permute-start.11
  43.5 5.4 %collective-permute-start.10 = (f32[1,16,128]{2,0,1:T(1,128)}, f32[1,16,128]{2,0,1:T(1,128)}, u32[]{:S(2)}, u32[]{:S(2)}) collective-permute-start(f32[1,16,128]{2,0,1:T(1,128)} %broadcast_select_fusion), channel_id=1, source_target_pairs={{0,1},{1,2},{2,3},{3,4},{4,5},{5,6},{6,7},{7,8},{8,9},{9,10},{10,1... | collective-permute-start | bytes 24584 | tf_op jit(solution)/shard_map/ppermute | solution.py:21
  49.0 0.7 gather_fusion.1
  49.7 3.2 fusion.74
  52.9 0.7 gather_fusion.2
  53.6 0.8 broadcast_select_fusion.4
  54.3 1.3 collective-permute-start.3
  55.6 6.1 %collective-permute-start.2 = (f32[2,16,128]{2,1,0:T(8,128)S(1)}, f32[2,16,128]{2,1,0:T(8,128)S(1)}, u32[]{:S(2)}, u32[]{:S(2)}) collective-permute-start(f32[2,16,128]{2,1,0:T(8,128)S(1)} %broadcast_select_fusion.4), channel_id=1, source_target_pairs={{0,1},{1,2},{2,3},{3,4},{4,5},{5,6},{6,7},{7,8},{8,9},{9,10},{10,1... | collective-permute-start | bytes 49160 | tf_op jit(solution)/shard_map/ppermute | solution.py:21
  61.8 0.7 pad_maximum_fusion.5
  62.5 1.3 gather_fusion.8
  63.9 0.7 gather_fusion.3
  64.6 2.6 fusion.75
  67.2 0.7 gather_fusion.4
  67.9 0.8 broadcast_select_fusion.3
  68.7 1.3 collective-permute-start.5
  70.0 7.4 %collective-permute-start.4 = (f32[2,16,128]{2,1,0:T(8,128)S(1)}, f32[2,16,128]{2,1,0:T(8,128)S(1)}, u32[]{:S(2)}, u32[]{:S(2)}) collective-permute-start(f32[2,16,128]{2,1,0:T(8,128)S(1)} %broadcast_select_fusion.3), channel_id=1, source_target_pairs={{0,1},{1,2},{2,3},{3,4},{4,5},{5,6},{6,7},{7,8},{8,9},{9,10},{10,1... | collective-permute-start | bytes 49160 | tf_op jit(solution)/shard_map/ppermute | solution.py:21
  77.4 1.9 fusion.21
  79.4 0.7 gather_fusion.5
  80.1 51.1 %all-gather.2.cloned.1.call-done = f32[1024,1024]{1,0:T(8,128)} async-done(((f32[64,1024]{1,0:T(8,128)}), f32[1024,1024]{1,0:T(8,128)}) %all-gather.2.cloned.1.call-update) | async-done | bytes 4194320 | tf_op jit(solution)/shard_map/all_gather | solution.py:83
  131.2 5.2 %copy.33 = f32[128,8,8,128]{3,2,1,0:T(8,128)} copy(f32[128,8,8,128]{3,1,2,0:T(8,128)} %bitcast.102) | data formatting | bytes 8388608
  136.4 352.5 %all-reduce.2.cloned.1.call-done = f32[8,16,128]{2,1,0:T(8,128)} async-done(((f32[8,16,128]{2,1,0:T(8,128)}), f32[8,16,128]{2,1,0:T(8,128)}) %all-reduce.2.cloned.1.call-update) | async-done | bytes 65552 | tf_op jit(solution)/shard_map/psum | solution.py:92
  488.9 6.2 %fusion = f32[16,8,128,1]{2,0,3,1:T(8,128)S(1)} fusion(f32[8,128,128,8]{2,3,1,0:T(8,128)} %bitcast.101, f32[8,16,128]{2,1,0:T(8,128)} %all-reduce.2.cloned.1.call-done), kind=kOutput, calls=%fused_computation.9 | convolution fusion | flops 201342976 | bytes 4325376 | tf_op jit(solution)/shard_map/ocb,cvb->vo/dot_general | solution.py:93
  495.6 2.5 fusion.8
  (60 shorter events, 1.0 us)
Async XLA Ops:
  7.4 42.4 %copy-start = (f32[4,8,128,128]{3,2,1,0:T(8,128)S(1)}, f32[4,8,128,128]{3,2,1,0:T(8,128)}, u32[]{:S(2)}) copy-start(f32[4,8,128,128]{3,2,1,0:T(8,128)} %param.19) | copy-start | bytes 6291460
  7.4 41.6 %copy-start.2 = (f32[4,16,128]{2,1,0:T(8,128)S(1)}, f32[4,16,128]{2,1,0:T(8,128)}, u32[]{:S(2)}) copy-start(f32[4,16,128]{2,1,0:T(8,128)} %param.18) | copy-start | bytes 98308
  7.4 32.6 %copy-start.1 = (f32[2,8,128,128]{3,2,1,0:T(8,128)S(1)}, f32[2,8,128,128]{3,2,1,0:T(8,128)}, u32[]{:S(2)}) copy-start(f32[2,8,128,128]{3,2,1,0:T(8,128)} %param.22) | copy-start | bytes 3145732
  7.4 123.8 %all-gather.2.cloned.1.call-start = ((), (), s32[]{:S(2)}) async-start(), calls=%async_computation.1 | async-start | bytes 4456448 | tf_op jit(solution)/shard_map/all_gather | solution.py:83
  8.1 480.8 %all-reduce.2.cloned.1.call-start = ((), (), s32[]{:S(2)}) async-start(), calls=%async_computation | async-start | bytes 131072 | tf_op jit(solution)/shard_map/psum | solution.py:92
  8.9 8.6 %copy-start.9 = (s32[1024]{0:T(1024)}, s32[1024]{0:T(1024)S(1)}, u32[]{:S(2)}) copy-start(s32[1024]{0:T(1024)S(1)} %pad_clamp_fusion.2) | copy-start | bytes 12292
  10.9 6.6 %copy-start.10 = (pred[2]{0:T(512)(128)(4,1)}, pred[2]{0:T(512)(128)(4,1)S(1)}, u32[]{:S(2)}) copy-start(pred[2]{0:T(512)(128)(4,1)S(1)} %compare_and_fusion.2) | copy-start | bytes 10
  10.9 38.0 %collective-permute-start.1 = (f32[2,16,128]{2,1,0:T(8,128)S(1)}, f32[2,16,128]{2,1,0:T(8,128)S(1)}, u32[]{:S(2)}, u32[]{:S(2)}) collective-permute-start(f32[2,16,128]{2,1,0:T(8,128)S(1)} %broadcast_select_fusion.5), channel_id=1, source_target_pairs={{1,0},{2,1},{3,2},{4,3},{5,4},{6,5},{7,6},{8,7},{9,8},{10,9},{11,1... | collective-permute-start | bytes 49160 | tf_op jit(solution)/shard_map/ppermute | solution.py:24
  12.2 36.7 %collective-permute-start = (f32[2,16,128]{2,1,0:T(8,128)S(1)}, f32[2,16,128]{2,1,0:T(8,128)S(1)}, u32[]{:S(2)}, u32[]{:S(2)}) collective-permute-start(f32[2,16,128]{2,1,0:T(8,128)S(1)} %broadcast_select_fusion.5), channel_id=1, source_target_pairs={{0,1},{1,2},{2,3},{3,4},{4,5},{5,6},{6,7},{7,8},{8,9},{9,10},{10,1... | collective-permute-start | bytes 49160 | tf_op jit(solution)/shard_map/ppermute | solution.py:21
  18.4 10.8 %collective-permute-start.7 = (f32[1,16,128]{2,0,1:T(1,128)S(1)}, f32[1,16,128]{2,0,1:T(1,128)S(1)}, u32[]{:S(2)}, u32[]{:S(2)}) collective-permute-start(f32[1,16,128]{2,0,1:T(1,128)S(1)} %broadcast_select_fusion.2), channel_id=1, source_target_pairs={{1,0},{2,1},{3,2},{4,3},{5,4},{6,5},{7,6},{8,7},{9,8},{10,9},{11,1... | collective-permute-start | bytes 24584 | tf_op jit(solution)/shard_map/ppermute | solution.py:24
  19.7 9.5 %collective-permute-start.6 = (f32[1,16,128]{2,0,1:T(1,128)S(1)}, f32[1,16,128]{2,0,1:T(1,128)S(1)}, u32[]{:S(2)}, u32[]{:S(2)}) collective-permute-start(f32[1,16,128]{2,0,1:T(1,128)S(1)} %broadcast_select_fusion.2), channel_id=1, source_target_pairs={{0,1},{1,2},{2,3},{3,4},{4,5},{5,6},{6,7},{7,8},{8,9},{9,10},{10,1... | collective-permute-start | bytes 24584 | tf_op jit(solution)/shard_map/ppermute | solution.py:21
  26.5 22.5 %copy-start.11 = (pred[2,8]{1,0:T(4,128)(4,1)}, pred[2,8]{1,0:T(4,128)(4,1)S(1)}, u32[]{:S(2)}) copy-start(pred[2,8]{1,0:T(4,128)(4,1)S(1)} %compare_and_fusion) | copy-start | bytes 52
  29.2 19.8 %copy-start.7 = (s32[1024]{0:T(1024)}, s32[1024]{0:T(1024)S(1)}, u32[]{:S(2)}) copy-start(s32[1024]{0:T(1024)S(1)} %pad_clamp_fusion) | copy-start | bytes 12292
  32.2 6.4 %collective-permute-start.9 = (f32[1,16,128]{2,0,1:T(1,128)S(1)}, f32[1,16,128]{2,0,1:T(1,128)S(1)}, u32[]{:S(2)}, u32[]{:S(2)}) collective-permute-start(f32[1,16,128]{2,0,1:T(1,128)S(1)} %broadcast_select_fusion.1), channel_id=1, source_target_pairs={{1,0},{2,1},{3,2},{4,3},{5,4},{6,5},{7,6},{8,7},{9,8},{10,9},{11,1... | collective-permute-start | bytes 24584 | tf_op jit(solution)/shard_map/ppermute | solution.py:24
  33.5 5.9 %collective-permute-start.8 = (f32[1,16,128]{2,0,1:T(1,128)S(1)}, f32[1,16,128]{2,0,1:T(1,128)S(1)}, u32[]{:S(2)}, u32[]{:S(2)}) collective-permute-start(f32[1,16,128]{2,0,1:T(1,128)S(1)} %broadcast_select_fusion.1), channel_id=1, source_target_pairs={{0,1},{1,2},{2,3},{3,4},{4,5},{5,6},{6,7},{7,8},{8,9},{9,10},{10,1... | collective-permute-start | bytes 24584 | tf_op jit(solution)/shard_map/ppermute | solution.py:21
  41.6 7.3 %copy-start.3 = (f32[2,16,128]{2,0,1:T(2,128)}, f32[2,16,128]{2,0,1:T(2,128)S(1)}, u32[]{:S(2)}) copy-start(f32[2,16,128]{2,0,1:T(2,128)S(1)} %get-tuple-element.20) | copy-start | bytes 49156
  42.2 19.5 %collective-permute-start.11 = (f32[1,16,128]{2,0,1:T(1,128)}, f32[1,16,128]{2,0,1:T(1,128)}, u32[]{:S(2)}, u32[]{:S(2)}) collective-permute-start(f32[1,16,128]{2,0,1:T(1,128)} %broadcast_select_fusion), channel_id=1, source_target_pairs={{1,0},{2,1},{3,2},{4,3},{5,4},{6,5},{7,6},{8,7},{9,8},{10,9},{11,1... | collective-permute-start | bytes 24584 | tf_op jit(solution)/shard_map/ppermute | solution.py:24
  43.5 18.2 %collective-permute-start.10 = (f32[1,16,128]{2,0,1:T(1,128)}, f32[1,16,128]{2,0,1:T(1,128)}, u32[]{:S(2)}, u32[]{:S(2)}) collective-permute-start(f32[1,16,128]{2,0,1:T(1,128)} %broadcast_select_fusion), channel_id=1, source_target_pairs={{0,1},{1,2},{2,3},{3,4},{4,5},{5,6},{6,7},{7,8},{8,9},{9,10},{10,1... | collective-permute-start | bytes 24584 | tf_op jit(solution)/shard_map/ppermute | solution.py:21
  49.7 12.0 %copy-start.4 = (f32[2,16,128]{2,0,1:T(2,128)S(1)}, f32[2,16,128]{2,0,1:T(2,128)}, u32[]{:S(2)}) copy-start(f32[2,16,128]{2,0,1:T(2,128)} %copy-done.3) | copy-start | bytes 49156
  54.3 9.5 %collective-permute-start.3 = (f32[2,16,128]{2,1,0:T(8,128)S(1)}, f32[2,16,128]{2,1,0:T(8,128)S(1)}, u32[]{:S(2)}, u32[]{:S(2)}) collective-permute-start(f32[2,16,128]{2,1,0:T(8,128)S(1)} %broadcast_select_fusion.4), channel_id=1, source_target_pairs={{1,0},{2,1},{3,2},{4,3},{5,4},{6,5},{7,6},{8,7},{9,8},{10,9},{11,1... | collective-permute-start | bytes 49160 | tf_op jit(solution)/shard_map/ppermute | solution.py:24
  55.6 8.2 %collective-permute-start.2 = (f32[2,16,128]{2,1,0:T(8,128)S(1)}, f32[2,16,128]{2,1,0:T(8,128)S(1)}, u32[]{:S(2)}, u32[]{:S(2)}) collective-permute-start(f32[2,16,128]{2,1,0:T(8,128)S(1)} %broadcast_select_fusion.4), channel_id=1, source_target_pairs={{0,1},{1,2},{2,3},{3,4},{4,5},{5,6},{6,7},{7,8},{8,9},{9,10},{10,1... | collective-permute-start | bytes 49160 | tf_op jit(solution)/shard_map/ppermute | solution.py:21
  68.7 10.7 %collective-permute-start.5 = (f32[2,16,128]{2,1,0:T(8,128)S(1)}, f32[2,16,128]{2,1,0:T(8,128)S(1)}, u32[]{:S(2)}, u32[]{:S(2)}) collective-permute-start(f32[2,16,128]{2,1,0:T(8,128)S(1)} %broadcast_select_fusion.3), channel_id=1, source_target_pairs={{1,0},{2,1},{3,2},{4,3},{5,4},{6,5},{7,6},{8,7},{9,8},{10,9},{11,1... | collective-permute-start | bytes 49160 | tf_op jit(solution)/shard_map/ppermute | solution.py:24
  70.0 9.4 %collective-permute-start.4 = (f32[2,16,128]{2,1,0:T(8,128)S(1)}, f32[2,16,128]{2,1,0:T(8,128)S(1)}, u32[]{:S(2)}, u32[]{:S(2)}) collective-permute-start(f32[2,16,128]{2,1,0:T(8,128)S(1)} %broadcast_select_fusion.3), channel_id=1, source_target_pairs={{0,1},{1,2},{2,3},{3,4},{4,5},{5,6},{6,7},{7,8},{8,9},{9,10},{10,1... | collective-permute-start | bytes 49160 | tf_op jit(solution)/shard_map/ppermute | solution.py:21
  488.8 6.2 %copy-start.5 = (f32[2,16,128]{2,0,1:T(2,128)S(1)}, f32[2,16,128]{2,0,1:T(2,128)}, u32[]{:S(2)}) copy-start(f32[2,16,128]{2,0,1:T(2,128)} %copy-done.3) | copy-start | bytes 49156
  488.9 6.2 %copy-start.6 = (f32[2,16,128]{2,0,1:T(2,128)S(1)}, f32[2,16,128]{2,0,1:T(2,128)}, u32[]{:S(2)}) copy-start(f32[2,16,128]{2,0,1:T(2,128)} %get-tuple-element.21) | copy-start | bytes 49156
  488.9 6.2 %copy-start.13 = (s32[2]{0:T(128)S(1)}, s32[2]{0:T(128)}, u32[]{:S(2)}) copy-start(s32[2]{0:T(128)} %param.26) | copy-start | bytes 28
  488.9 6.5 %copy-start.12 = (s32[4]{0:T(128)S(1)}, s32[4]{0:T(128)}, u32[]{:S(2)}) copy-start(s32[4]{0:T(128)} %param.25) | copy-start | bytes 52
  488.9 6.7 %copy-start.8 = (pred[4,8]{1,0:T(4,128)(4,1)S(1)}, pred[4,8]{1,0:T(4,128)(4,1)}, u32[]{:S(2)}) copy-start(pred[4,8]{1,0:T(4,128)(4,1)} %compare_and_fusion.1) | copy-start | bytes 100
Sparse Core Ops, SparseCore 0:
  11.5 119.6 all-gather.1
Sparse Core Ops, SparseCore 1:
  25.8 462.9 all-reduce.1
where the time goes:
time: 507 us; the launch traced here: 506 us
  waiting for transfers between devices  405 us (80%)
  starting transfers between devices  40.4 us (8%)
  matrix products  21.8 us (4%)
  between operations  15.9 us (3%)
  local copies, waits for them, and re-layouts  13.3 us (3%)
  other arithmetic  9.03 us (2%)
    psum x1, waiting for transfers between devices, shards(): coarse_res = coarse_weight * lax.psum(coarse_part, 'dom')  352 us
    all_gather x1, waiting for transfers between devices, shards(): lax.all_gather(coarse_inverse, 'level', axis=0, tiled=True)  51.1 us
    ppermute x6, starting transfers between devices, padded(): lax.ppermute(lax.slice_in_dim(block, block.shape[dim] - width, None, axis...  32.6 us
    dot_general x6, matrix products, boundary_apply(): jnp.einsum('rkab,rkvb->rva', blocks, picked, precision=lax.Precision.HIGH...  13.4 us
  transfers between devices with their start and end apart: 14, of which 3 were waited for; matrix products, arithmetic and copies ran while one was open for 7% of the time, Pallas kernels for 0%

commit v1 on v0

v1 whole, which is shorter than its diff:
```python
import jax
import jax.numpy as jnp
from jax import lax
from jax.experimental import pallas as pl
from jax.experimental.pallas import tpu as pltpu
from jax.sharding import PartitionSpec as P

CAGG = 8
DEG = 4
CENTRE = 1.0
HALF_WIDTH = 0.7
DAMPING = 0.7
MID_WEIGHT = 0.5**0.5
COARSE_WEIGHT = CAGG**-0.5

F32 = jnp.float32
BF16 = jnp.bfloat16


def sweep_constants():
    ratio = CENTRE / HALF_WIDTH
    rho_prev = 1.0 / ratio
    constants = []
    for _ in range(DEG - 1):
        rho_next = 1.0 / (2.0 * ratio - rho_prev)
        constants.append((rho_next * rho_prev, 2.0 * rho_next / HALF_WIDTH))
        rho_prev = rho_next
    return constants


def split(value):
    high = value.astype(BF16)
    low = (value - high.astype(F32)).astype(BF16)
    return high, low


def product(left, right):
    full = lax.dot_general(left, right, (((1,), (1,)), ((), ())), preferred_element_type=F32)
    return full[:16, :128] + (full[:16, 128:] + full[16:, :128])


def wait_for(ref, sem):
    pltpu.make_async_copy(ref, ref, sem).wait()


def kernel(
    fine_cols,
    fine_edges,
    mid_cols,
    mid_edges,
    fine_map,
    mid_map,
    source_hbm,
    fine_hbm,
    mid_hbm,
    inverse_hbm,
    out,
    source,
    fine_raw,
    mid_raw,
    fine_w,
    mid_w,
    fine_e,
    fine_d,
    mid_g,
    mid_e,
    mid_d,
    fine_x,
    mid_x,
    halo_out,
    halo_in,
    raw_out,
    raw_in,
    res_out,
    res_in,
    inv_in,
    inv_w,
    corr_out,
    corr_in,
    final,
    picked,
    joined,
    load_sem,
    halo_send,
    halo_recv,
    raw_send,
    raw_recv,
    inv_send,
    inv_recv,
    res_send,
    res_recv,
    corr_send,
    corr_recv,
    z_send,
    z_recv,
    x_send,
    x_recv,
):
    level = lax.axis_index("level")
    dom = lax.axis_index("dom")
    half = level // 8
    mine = level % 8
    y_pos = mine // 2
    core = level % 2
    z_pos = dom // 4
    x_pos = dom % 4
    centre = (z_pos == 3) | (z_pos == 4)
    centre_i = jnp.where(centre, 1, 0)
    z_two = jnp.where(z_pos == 4, 1, 0)
    has_low = dom > 0
    has_high = dom < 31
    import_z = jnp.where(z_pos == 7, 3, 4)
    imports = (z_pos == 0) | (z_pos == 7)

    def remote(src, dst, send, recv, to_level, to_dom):
        return pltpu.make_async_remote_copy(
            src_ref=src,
            dst_ref=dst,
            send_sem=send,
            recv_sem=recv,
            device_id=(to_level, to_dom),
            device_id_type=pl.DeviceIdType.MESH,
        )

    load_source = pltpu.make_async_copy(source_hbm, source, load_sem.at[0])
    load_source.start()
    load_fine = [
        pltpu.make_async_copy(fine_hbm.at[r], fine_raw.at[r], load_sem.at[1 + r]) for r in range(4)
    ]
    load_mid = [
        pltpu.make_async_copy(mid_hbm.at[r], mid_raw.at[r], load_sem.at[5 + r]) for r in range(2)
    ]
    for load in load_fine + load_mid:
        load.start()

    barrier = pltpu.get_barrier_semaphore()

    def greet(to_level, to_dom):
        pl.semaphore_signal(
            barrier, inc=1, device_id=(to_level, to_dom), device_id_type=pl.DeviceIdType.MESH
        )

    @pl.when(has_low)
    def _():
        greet(level, dom - 1)

    @pl.when(has_high)
    def _():
        greet(level, dom + 1)

    for other_z in (3, 4):

        @pl.when(z_pos != other_z)
        def _():
            greet(level, other_z * 4 + x_pos)

    for step in range(1, 4):
        greet(level, z_pos * 4 + (x_pos + step) % 4)

    @pl.when(centre)
    def _():
        @pl.loop(1, 32)
        def _(step):
            greet(level, (dom + step) % 32)

        @pl.loop(1, 8)
        def _(step):
            greet(half * 8 + (mine + step) % 8, dom)

        @pl.when(core == 0)
        def _():
            greet(level + 1, dom)

        @pl.when(core == 1)
        def _():
            from_dom = jnp.where(z_pos == 3, 7, 0) * 4 + x_pos
            greet((1 - half) * 8 + y_pos * 2, from_dom)
            greet((1 - half) * 8 + y_pos * 2 + 1, from_dom)

    load_source.wait()
    lanes = lax.broadcasted_iota(jnp.int32, (1, 128), 1)
    for j in range(2):
        total = None
        for i in range(4):
            term = jnp.where(fine_map[i] == j, source[i], 0.0)
            total = term if total is None else total + term
        mid_g[j] = MID_WEIGHT * total
    raw_out[:, 6:8, :] = jnp.zeros((8, 2, 128), F32)
    for j in range(2):
        row = jnp.where((lanes < 16) & (lanes % 8 == mid_map[j]), 1.0, 0.0)
        for n in range(8):
            first = 4 * (n % 4) + 2 * (n // 4)
            raw_out[n, 2 * j : 2 * j + 2, :] = mid_g[j, first : first + 2, :]
            raw_out[n, 4 + j : 5 + j, :] = row

    def fill_halo(turn, fine_ref, mid_ref):
        halo_out[turn, 0] = fine_ref[fine_edges[0]]
        halo_out[turn, 1] = fine_ref[fine_edges[1]]
        halo_out[turn, 2] = mid_ref[mid_edges[0]]

    fill_halo(0, source, mid_g)

    @pl.when(dom == 0)
    def _():
        for turn in range(3):
            halo_in[turn, 0] = jnp.zeros((3, 16, 128), F32)

    @pl.when(dom == 31)
    def _():
        for turn in range(3):
            halo_in[turn, 1] = jnp.zeros((3, 16, 128), F32)

    sides = jnp.where(has_low, 1, 0) + jnp.where(has_high, 1, 0)
    waits = sides + 8 - centre_i + 3 + 14 * centre_i
    waits = waits + jnp.where(imports, 1, 0) + centre_i * core
    pl.semaphore_wait(barrier, waits)

    def halo_low(turn):
        return remote(
            halo_out.at[turn],
            halo_in.at[turn, 1],
            halo_send.at[turn, 0],
            halo_recv.at[turn, 1],
            level,
            dom - 1,
        )

    def halo_high(turn):
        return remote(
            halo_out.at[turn],
            halo_in.at[turn, 0],
            halo_send.at[turn, 1],
            halo_recv.at[turn, 0],
            level,
            dom + 1,
        )

    def start_halo(turn):
        @pl.when(has_low)
        def _():
            halo_low(turn).start()

        @pl.when(has_high)
        def _():
            halo_high(turn).start()

    def wait_halo(turn):
        @pl.when(has_low)
        def _():
            wait_for(halo_in.at[turn, 0], halo_recv.at[turn, 0])

        @pl.when(has_high)
        def _():
            wait_for(halo_in.at[turn, 1], halo_recv.at[turn, 1])

    start_halo(0)

    @pl.loop(0, 8)
    def _(n):
        to_dom = (3 + n // 4) * 4 + n % 4

        @pl.when(to_dom != dom)
        def _():
            remote(raw_out.at[n], raw_in.at[dom], raw_send, raw_recv, level, to_dom).start()

        @pl.when(to_dom == dom)
        def _():
            pltpu.make_async_copy(raw_out.at[n], raw_in.at[dom], raw_recv).start()

    @pl.when(centre & (core == 0))
    def _():
        pltpu.make_async_copy(inverse_hbm, inv_in.at[0], inv_recv).start()

    @pl.when(centre & (core == 1))
    def _():
        remote(inverse_hbm, inv_in.at[1], inv_send, inv_recv, level - 1, dom).start()

    @pl.when(imports)
    def _():
        remote(
            inverse_hbm,
            inv_in.at[core],
            inv_send,
            inv_recv,
            (1 - half) * 8 + y_pos * 2 + 1,
            import_z * 4 + x_pos,
        ).start()

    for r in range(4):
        load_fine[r].wait()
        for k in range(8):
            high, low = split(fine_raw[r, k])
            fine_w[r, 0:128, k * 128 : k * 128 + 128] = high
            fine_w[r, 128:256, k * 128 : k * 128 + 128] = low
    for r in range(2):
        load_mid[r].wait()
        for k in range(8):
            high, low = split(mid_raw[r, k])
            mid_w[r, 0:128, k * 128 : k * 128 + 128] = high
            mid_w[r, 128:256, k * 128 : k * 128 + 128] = low

    def put(ref, slot, value):
        high, low = split(value)
        ref[slot, 0:16, :] = high
        ref[slot, 16:32, :] = low

    constants = sweep_constants()

    def sweep(turn):
        keep, push = constants[turn]
        old_fine = source if turn == 0 else fine_e
        old_mid = mid_g if turn == 0 else mid_e
        old_fine_d = source if turn == 0 else fine_d
        old_mid_d = mid_g if turn == 0 else mid_d
        for r in range(4):
            put(fine_x, r, old_fine[r])
        for r in range(2):
            put(mid_x, r, old_mid[r])
        wait_halo(turn)
        for side in range(2):
            for row in range(2):
                put(fine_x, 4 + 2 * side + row, halo_in[turn, side, row])
            put(mid_x, 2 + side, halo_in[turn, side, 2])
        for r in range(4):
            left = jnp.concatenate([fine_x[fine_cols[r, k]] for k in range(8)], axis=1)
            applied = old_fine[r] + product(left, fine_w[r])
            step = keep * old_fine_d[r] + push * (source[r] - applied)
            fine_d[r] = step
            fine_e[r] = old_fine[r] + step
        for r in range(2):
            left = jnp.concatenate([mid_x[mid_cols[r, k]] for k in range(8)], axis=1)
            applied = old_mid[r] + product(left, mid_w[r])
            step = keep * old_mid_d[r] + push * (mid_g[r] - applied)
            mid_d[r] = step
            mid_e[r] = old_mid[r] + step
        if turn < 2:
            fill_halo(turn + 1, fine_e, mid_e)
            start_halo(turn + 1)

    sweep(0)

    @pl.when(centre)
    def _():
        wait_for(raw_in, raw_recv)
        rows = lax.broadcasted_iota(jnp.int32, (32, 8, 128), 1)
        cols = lax.broadcasted_iota(jnp.int32, (32, 8, 128), 2)
        value = raw_in[...]
        first = jnp.broadcast_to(value[:, 4:5, :], (32, 8, 128))
        second = jnp.broadcast_to(value[:, 5:6, :], (32, 8, 128))
        picks = jnp.where(rows < 2, first, second)
        wanted = (rows < 4) & (cols // 8 == rows % 2)
        picks = jnp.where(wanted, picks, 0.0).reshape(256, 128).astype(BF16)
        high, low = split(value.reshape(256, 128))
        both = jnp.concatenate([high, low], axis=1)
        full = lax.dot_general(picks, both, (((0,), (0,)), ((), ())), preferred_element_type=F32)
        total = full[:16, :128] + full[:16, 128:]
        res_out[...] = total

        @pl.loop(0, 8)
        def _(peer):
            @pl.when(peer != mine)
            def _():
                remote(res_out, res_in.at[mine], res_send, res_recv, half * 8 + peer, dom).start()

            @pl.when(peer == mine)
            def _():
                pltpu.make_async_copy(res_out, res_in.at[mine], res_recv).start()

    sweep(1)

    @pl.when(centre)
    def _():
        wait_for(inv_in, inv_recv)
        for h in range(2):
            high, low = split(inv_in[h])
            inv_w[64 * h : 64 * h + 64, :] = high
            inv_w[128 + 64 * h : 192 + 64 * h, :] = low
        wait_for(res_in, res_recv)
        parts = []
        for c in range(8):
            block = jnp.concatenate([res_in[:, c, :], res_in[:, 8 + c, :]], axis=0)
            high, low = split(block)
            parts.append(jnp.concatenate([high, low], axis=0))
        left = jnp.concatenate(parts, axis=1)
        corr = product(left, inv_w[...])
        for peer in range(8):
            corr_out[peer, 0:1, :] = corr[peer : peer + 1, :]
            corr_out[peer, 1:2, :] = corr[8 + peer : 9 + peer, :]
        row = jnp.where(core == 0, half, 1 - half) * 4 + y_pos

        @pl.loop(0, 8)
        def _(peer):
            @pl.when(peer != mine)
            def _():
                remote(
                    corr_out.at[peer], corr_in.at[row], corr_send, corr_recv, half * 8 + peer, dom
                ).start()

            @pl.when(peer == mine)
            def _():
                pltpu.make_async_copy(corr_out.at[peer], corr_in.at[row], corr_recv).start()

    sweep(2)

    @pl.when(centre)
    def _():
        wait_for(corr_in, corr_recv)

        @pl.loop(0, 8)
        def _(other_z):
            @pl.when(other_z != z_pos)
            def _():
                remote(
                    corr_in,
                    final.at[x_pos, z_two],
                    z_send,
                    z_recv,
                    level,
                    other_z * 4 + x_pos,
                ).start()

            @pl.when(other_z == z_pos)
            def _():
                pltpu.make_async_copy(corr_in, final.at[x_pos, z_two], z_recv).start()

    wait_for(final.at[0], z_recv)

    for step in range(1, 4):
        remote(
            final.at[x_pos],
            final.at[x_pos],
            x_send,
            x_recv,
            level,
            z_pos * 4 + (x_pos + step) % 4,
        ).start()
    wait_for(final.at[pl.ds(0, 3)], x_recv)

    for j in range(2):
        for n in range(8):
            first = 4 * (n // 2) + 2 * (n % 2)
            picked[first : first + 2, :] = final[n // 2, n % 2, mid_map[j]]
        joined[j] = mid_e[j] + (COARSE_WEIGHT * COARSE_WEIGHT) * picked[...]
    for i in range(4):
        out[i] = DAMPING * (fine_e[i] + MID_WEIGHT * joined[fine_map[i]])

    for turn in range(3):

        @pl.when(has_low)
        def _():
            wait_for(halo_out.at[turn], halo_send.at[turn, 0])

        @pl.when(has_high)
        def _():
            wait_for(halo_out.at[turn], halo_send.at[turn, 1])

    wait_for(final.at[pl.ds(0, 3)], x_send)

    @pl.when(imports | (centre & (core == 1)))
    def _():
        wait_for(inverse_hbm, inv_send)

    @pl.when(jnp.logical_not(centre))
    def _():
        wait_for(raw_out, raw_send)

    @pl.when(centre)
    def _():
        wait_for(raw_out.at[pl.ds(0, 7)], raw_send)
        wait_for(res_in.at[pl.ds(0, 7)], res_send)
        wait_for(corr_out.at[pl.ds(0, 7)], corr_send)
        wait_for(raw_in.at[pl.ds(0, 14)], z_send)


def shards(
    right_side,
    fine_blocks,
    fine_cols,
    fine_edges,
    mid_blocks,
    mid_cols,
    mid_edges,
    fine_map,
    mid_map,
    coarse_inverse,
):
    smem = pl.BlockSpec(memory_space=pltpu.SMEM)
    anywhere = pl.BlockSpec(memory_space=pl.ANY)
    vmem = pltpu.VMEM
    dma = pltpu.SemaphoreType.DMA
    return pl.pallas_call(
        kernel,
        out_shape=jax.ShapeDtypeStruct(right_side.shape, F32),
        in_specs=[smem] * 6 + [anywhere] * 4,
        out_specs=pl.BlockSpec(memory_space=vmem),
        scratch_shapes=[
            vmem((4, 16, 128), F32),
            vmem((4, 8, 128, 128), F32),
            vmem((2, 8, 128, 128), F32),
            vmem((4, 256, 1024), BF16),
            vmem((2, 256, 1024), BF16),
            vmem((4, 16, 128), F32),
            vmem((4, 16, 128), F32),
            vmem((2, 16, 128), F32),
            vmem((2, 16, 128), F32),
            vmem((2, 16, 128), F32),
            vmem((8, 32, 128), BF16),
            vmem((4, 32, 128), BF16),
            vmem((3, 3, 16, 128), F32),
            vmem((3, 2, 3, 16, 128), F32),
            vmem((8, 8, 128), F32),
            vmem((32, 8, 128), F32),
            vmem((16, 128), F32),
            vmem((8, 16, 128), F32),
            vmem((2, 64, 1024), F32),
            vmem((256, 1024), BF16),
            vmem((8, 2, 128), F32),
            vmem((8, 2, 128), F32),
            vmem((4, 2, 8, 2, 128), F32),
            vmem((16, 128), F32),
            vmem((2, 16, 128), F32),
            dma((7,)),
            dma((3, 2)),
            dma((3, 2)),
            dma,
            dma,
            dma,
            dma,
            dma,
            dma,
            dma,
            dma,
            dma,
            dma,
            dma,
            dma,
        ],
        compiler_params=pltpu.CompilerParams(
            collective_id=0, has_side_effects=True, vmem_limit_bytes=40 * 1024 * 1024
        ),
    )(
        fine_cols,
        fine_edges,
        mid_cols,
        mid_edges,
        fine_map,
        mid_map,
        right_side,
        fine_blocks,
        mid_blocks,
        coarse_inverse,
    )


def solution(mesh):
    in_specs = (
        P("dom", "level", None),
        P("dom", None, None, None),
        P("dom", None),
        P("dom"),
        P("dom", None, None, None),
        P("dom", None),
        P("dom"),
        P("dom"),
        P("dom"),
        P("level", None),
    )
    out_specs = P("dom", "level", None)
    return jax.shard_map(shards, mesh=mesh, in_specs=in_specs, out_specs=out_specs, check_vma=False)
```

time: 507 us -> 50.1 us (0.10)
  the two profiles are of different devices: /device:TPU:8 before, /device:TPU:1 now
where the time goes in v1:
time: 50.1 us; the launch traced here: 49.3 us
  Pallas kernels  40.1 us (80%)
  local copies, waits for them, and re-layouts  8.46 us (17%)
  between operations  0.68 us (1%)
    pallas_call x1, Pallas kernels, shards(): pl.pallas_call(kernel, out_shape=jax.ShapeDtypeStruct(right_side.shape, F...  40.1 us
    unnamed x19, local copies, waits for them, and re-layouts  8.46 us

profile of v1, /device:TPU:1, one launch (start us, length us, event | category | flops | bytes accessed | tf_op | source)
XLA Modules:
  0.0 49.3 jit_solution(11970387335392928224)
XLA Ops:
  0.7 0.0 copy-start
  0.7 1.6 %copy-done = f32[4,8,128,128]{3,2,1,0:T(8,128)S(1)} copy-done((f32[4,8,128,128]{3,2,1,0:T(8,128)S(1)}, f32[4,8,128,128]{3,2,1,0:T(8,128)}, u32[]{:S(2)}) %copy-start) | copy-done | bytes 2097176
  2.2 0.0 copy-start.1
  2.2 1.2 %copy-done.1 = f32[2,8,128,128]{3,2,1,0:T(8,128)S(1)} copy-done((f32[2,8,128,128]{3,2,1,0:T(8,128)S(1)}, f32[2,8,128,128]{3,2,1,0:T(8,128)}, u32[]{:S(2)}) %copy-start.1) | copy-done | bytes 1048600
  3.5 0.0 copy-start.2
  3.5 0.9 %copy-done.2 = f32[64,1024]{1,0:T(8,128)S(1)} copy-done((f32[64,1024]{1,0:T(8,128)S(1)}, f32[64,1024]{1,0:T(8,128)}, u32[]{:S(2)}) %copy-start.2) | copy-done | bytes 262168
  4.4 0.0 copy-start.3
  4.4 0.8 %copy-done.3 = f32[4,16,128]{2,1,0:T(8,128)S(1)} copy-done((f32[4,16,128]{2,1,0:T(8,128)S(1)}, f32[4,16,128]{2,1,0:T(8,128)}, u32[]{:S(2)}) %copy-start.3) | copy-done | bytes 32792
  5.2 0.0 copy-start.4
  5.2 0.7 %copy-done.4 = s32[4,8]{1,0:T(4,128)S(1)} copy-done((s32[4,8]{1,0:T(4,128)S(1)}, s32[4,8]{1,0:T(4,128)}, u32[]{:S(2)}) %copy-start.4) | copy-done | bytes 152
  5.9 0.0 copy-start.5
  5.9 0.7 %copy-done.5 = s32[2,8]{1,0:T(2,128)S(1)} copy-done((s32[2,8]{1,0:T(2,128)S(1)}, s32[2,8]{1,0:T(2,128)}, u32[]{:S(2)}) %copy-start.5) | copy-done | bytes 88
  6.5 0.0 copy-start.6
  6.5 0.7 %copy-done.6 = s32[2]{0:T(128)S(1)} copy-done((s32[2]{0:T(128)S(1)}, s32[2]{0:T(128)}, u32[]{:S(2)}) %copy-start.6) | copy-done | bytes 32
  7.2 0.0 copy-start.7
  7.2 0.7 %copy-done.7 = s32[4]{0:T(128)S(1)} copy-done((s32[4]{0:T(128)S(1)}, s32[4]{0:T(128)}, u32[]{:S(2)}) %copy-start.7) | copy-done | bytes 40
  7.9 0.0 copy-start.8
  7.9 0.7 %copy-done.8 = s32[2]{0:T(128)S(1)} copy-done((s32[2]{0:T(128)S(1)}, s32[2]{0:T(128)}, u32[]{:S(2)}) %copy-start.8) | copy-done | bytes 32
  8.5 40.1 %shard_map.100 = f32[4,16,128]{2,1,0:T(8,128)S(1)} custom-call(s32[4,8]{1,0:T(4,128)S(1)} %copy-done.4, s32[2]{0:T(128)S(1)} %copy-done.6, s32[2,8]{1,0:T(2,128)S(1)} %copy-done.5, s32[1]{0:T(128)S(6)} %copy.12.mid_edges, s32[4]{0:T(128)S(1)} %copy-done.7, s32[2]{0:T(128)S(1)} %copy-done.8, f32[4,16,128]{2,1,0:T(8,128)S(1)} %copy-done.3, ...), custom_call_target="tpu_custom_call" | custom-call | tf_op jit(solution)/shard_map/pallas_call | solution.py:491
  48.6 0.6 %copy.13 = f32[4,16,128]{2,1,0:T(8,128)} copy(f32[4,16,128]{2,1,0:T(8,128)S(1)} %shard_map.100) | data formatting | bytes 65536
Async XLA Ops:
  0.7 1.6 %copy-start = (f32[4,8,128,128]{3,2,1,0:T(8,128)S(1)}, f32[4,8,128,128]{3,2,1,0:T(8,128)}, u32[]{:S(2)}) copy-start(f32[4,8,128,128]{3,2,1,0:T(8,128)} %fine_hbm.1) | copy-start | bytes 6291460
  2.2 1.2 %copy-start.1 = (f32[2,8,128,128]{3,2,1,0:T(8,128)S(1)}, f32[2,8,128,128]{3,2,1,0:T(8,128)}, u32[]{:S(2)}) copy-start(f32[2,8,128,128]{3,2,1,0:T(8,128)} %mid_hbm.1) | copy-start | bytes 3145732
  3.5 0.9 %copy-start.2 = (f32[64,1024]{1,0:T(8,128)S(1)}, f32[64,1024]{1,0:T(8,128)}, u32[]{:S(2)}) copy-start(f32[64,1024]{1,0:T(8,128)} %inverse_hbm.1) | copy-start | bytes 786436
  4.4 0.8 %copy-start.3 = (f32[4,16,128]{2,1,0:T(8,128)S(1)}, f32[4,16,128]{2,1,0:T(8,128)}, u32[]{:S(2)}) copy-start(f32[4,16,128]{2,1,0:T(8,128)} %source_hbm.1) | copy-start | bytes 98308
  5.2 0.7 %copy-start.4 = (s32[4,8]{1,0:T(4,128)S(1)}, s32[4,8]{1,0:T(4,128)}, u32[]{:S(2)}) copy-start(s32[4,8]{1,0:T(4,128)} %fine_cols.1) | copy-start | bytes 388
  5.9 0.7 %copy-start.5 = (s32[2,8]{1,0:T(2,128)S(1)}, s32[2,8]{1,0:T(2,128)}, u32[]{:S(2)}) copy-start(s32[2,8]{1,0:T(2,128)} %mid_cols.1) | copy-start | bytes 196
  6.5 0.7 %copy-start.6 = (s32[2]{0:T(128)S(1)}, s32[2]{0:T(128)}, u32[]{:S(2)}) copy-start(s32[2]{0:T(128)} %fine_edges.1) | copy-start | bytes 28
  7.2 0.7 %copy-start.7 = (s32[4]{0:T(128)S(1)}, s32[4]{0:T(128)}, u32[]{:S(2)}) copy-start(s32[4]{0:T(128)} %fine_map.1) | copy-start | bytes 52
  7.9 0.7 %copy-start.8 = (s32[2]{0:T(128)S(1)}, s32[2]{0:T(128)}, u32[]{:S(2)}) copy-start(s32[2]{0:T(128)} %mid_map.1) | copy-start | bytes 28

commit v2 on v1

--- a/solution.py
+++ b/solution.py
@@ -44,17 +44,23 @@
 
 
 def kernel(
+    fine_cols_hbm,
+    fine_edges_hbm,
+    mid_cols_hbm,
+    mid_edges_hbm,
+    fine_map_hbm,
+    mid_map_hbm,
+    source_hbm,
+    fine_hbm,
+    mid_hbm,
+    inverse_hbm,
+    out,
     fine_cols,
     fine_edges,
     mid_cols,
     mid_edges,
     fine_map,
     mid_map,
-    source_hbm,
-    fine_hbm,
-    mid_hbm,
-    inverse_hbm,
-    out,
     source,
     fine_raw,
     mid_raw,
@@ -122,8 +128,23 @@
             device_id_type=pl.DeviceIdType.MESH,
         )
 
+    load_small = [
+        pltpu.make_async_copy(src, dst, load_sem.at[7 + n])
+        for n, (src, dst) in enumerate(
+            [
+                (fine_map_hbm, fine_map),
+                (mid_map_hbm, mid_map),
+                (fine_edges_hbm, fine_edges),
+                (mid_edges_hbm, mid_edges),
+                (fine_cols_hbm, fine_cols),
+                (mid_cols_hbm, mid_cols),
+            ]
+        )
+    ]
     load_source = pltpu.make_async_copy(source_hbm, source, load_sem.at[0])
     load_source.start()
+    for load in load_small:
+        load.start()
     load_fine = [
         pltpu.make_async_copy(fine_hbm.at[r], fine_raw.at[r], load_sem.at[1 + r]) for r in range(4)
     ]
@@ -177,6 +198,8 @@
             greet((1 - half) * 8 + y_pos * 2, from_dom)
             greet((1 - half) * 8 + y_pos * 2 + 1, from_dom)
 
+    for load in load_small:
+        load.wait()
     load_source.wait()
     lanes = lax.broadcasted_iota(jnp.int32, (1, 128), 1)
     for j in range(2):
@@ -484,16 +507,22 @@
     mid_map,
     coarse_inverse,
 ):
-    smem = pl.BlockSpec(memory_space=pltpu.SMEM)
-    anywhere = pl.BlockSpec(memory_space=pl.ANY)
+    hbm = pl.BlockSpec(memory_space=pltpu.HBM)
+    smem = pltpu.SMEM
     vmem = pltpu.VMEM
     dma = pltpu.SemaphoreType.DMA
     return pl.pallas_call(
         kernel,
         out_shape=jax.ShapeDtypeStruct(right_side.shape, F32),
-        in_specs=[smem] * 6 + [anywhere] * 4,
+        in_specs=[hbm] * 10,
         out_specs=pl.BlockSpec(memory_space=vmem),
         scratch_shapes=[
+            smem((4, 8), jnp.int32),
+            smem((2,), jnp.int32),
+            smem((2, 8), jnp.int32),
+            smem((1,), jnp.int32),
+            smem((4,), jnp.int32),
+            smem((2,), jnp.int32),
             vmem((4, 16, 128), F32),
             vmem((4, 8, 128, 128), F32),
             vmem((2, 8, 128, 128), F32),
@@ -519,7 +548,7 @@
             vmem((4, 2, 8, 2, 128), F32),
             vmem((16, 128), F32),
             vmem((2, 16, 128), F32),
-            dma((7,)),
+            dma((13,)),
             dma((3, 2)),
             dma((3, 2)),
             dma,
@@ -536,7 +565,7 @@
             dma,
         ],
         compiler_params=pltpu.CompilerParams(
-            collective_id=0, has_side_effects=True, vmem_limit_bytes=40 * 1024 * 1024
+            collective_id=0, has_side_effects=True, vmem_limit_bytes=67043328
         ),
     )(
         fine_cols,

time: 50.1 us -> 41.7 us (0.83); the launches traced: 49.3 us -> 41.4 us
  local copies, waits for them, and re-layouts: 8.46 us -> 1.38 us
  Pallas kernels: 40.1 us -> 39.4 us
    unnamed x19 -> x1, local copies, waits for them, and re-layouts: 8.46 us -> 1.38 us
    pallas_call x1, Pallas kernels: 40.1 us -> 39.4 us  [shards(): pl.pallas_call(kernel, out_shape=jax.ShapeDtypeStruct(right_side.shape, F...]
where the time goes in v2:
time: 41.7 us; the launch traced here: 41.4 us
  Pallas kernels  39.4 us (94%)
  local copies, waits for them, and re-layouts  1.38 us (3%)
  between operations  0.66 us (2%)
    pallas_call x1, Pallas kernels, shards(): pl.pallas_call(kernel, out_shape=jax.ShapeDtypeStruct(right_side.shape, F...  39.4 us
    unnamed x1, local copies, waits for them, and re-layouts  1.38 us

profile of v2, /device:TPU:1, one launch (start us, length us, event | category | flops | bytes accessed | tf_op | source)
XLA Modules:
  0.0 41.4 jit_solution(3970545659153642679)
XLA Ops:
  0.7 39.4 %shard_map.100 = f32[4,16,128]{2,1,0:T(8,128)} custom-call(s32[4,8]{1,0:T(4,128)} %fine_cols_hbm.1, s32[2]{0:T(128)} %fine_edges_hbm.1, s32[2,8]{1,0:T(2,128)} %mid_cols_hbm.1, s32[1]{0:T(128)S(6)} %copy.12.mid_edges_hbm, s32[4]{0:T(128)} %fine_map_hbm.1, s32[2]{0:T(128)} %mid_map_hbm.1, f32[4,16,128]{2,1,0:T(8,128)} %source_hbm.1, ...), custom_call_target="tpu_custom_call" | custom-call | tf_op jit(solution)/shard_map/pallas_call | solution.py:514
  40.0 1.4 %copy.13 = f32[4,16,128]{2,1,0:T(8,128)} copy(f32[4,16,128]{2,1,0:T(8,128)} %shard_map.100) | data formatting | bytes 65536

commit v3 on v2

--- a/solution.py
+++ b/solution.py
@@ -82,7 +82,7 @@
     inv_in,
     inv_w,
     corr_out,
-    corr_in,
+    spare,
     final,
     picked,
     joined,
@@ -95,8 +95,6 @@
     inv_recv,
     res_send,
     res_recv,
-    corr_send,
-    corr_recv,
     z_send,
     z_recv,
     x_send,
@@ -170,10 +168,11 @@
         greet(level, dom + 1)
 
     for other_z in (3, 4):
-
-        @pl.when(z_pos != other_z)
-        def _():
-            greet(level, other_z * 4 + x_pos)
+        for peer in range(8):
+
+            @pl.when((z_pos != other_z) | (mine != peer))
+            def _():
+                greet(half * 8 + peer, other_z * 4 + x_pos)
 
     for step in range(1, 4):
         greet(level, z_pos * 4 + (x_pos + step) % 4)
@@ -183,10 +182,6 @@
         @pl.loop(1, 32)
         def _(step):
             greet(level, (dom + step) % 32)
-
-        @pl.loop(1, 8)
-        def _(step):
-            greet(half * 8 + (mine + step) % 8, dom)
 
         @pl.when(core == 0)
         def _():
@@ -208,13 +203,13 @@
             term = jnp.where(fine_map[i] == j, source[i], 0.0)
             total = term if total is None else total + term
         mid_g[j] = MID_WEIGHT * total
-    raw_out[:, 6:8, :] = jnp.zeros((8, 2, 128), F32)
-    for j in range(2):
-        row = jnp.where((lanes < 16) & (lanes % 8 == mid_map[j]), 1.0, 0.0)
-        for n in range(8):
-            first = 4 * (n % 4) + 2 * (n // 4)
+    wanted = jnp.where(lanes < 64, mid_map[0], mid_map[1])
+    row = jnp.where((lanes % 64 < 16) & (lanes % 8 == wanted), 1.0, 0.0)
+    for n in range(8):
+        first = 4 * (n % 4) + 2 * (n // 4)
+        for j in range(2):
             raw_out[n, 2 * j : 2 * j + 2, :] = mid_g[j, first : first + 2, :]
-            raw_out[n, 4 + j : 5 + j, :] = row
+        raw_out[n, 4:5, :] = row
 
     def fill_halo(turn, fine_ref, mid_ref):
         halo_out[turn, 0] = fine_ref[fine_edges[0]]
@@ -233,8 +228,12 @@
         for turn in range(3):
             halo_in[turn, 1] = jnp.zeros((3, 16, 128), F32)
 
+    @pl.when(centre)
+    def _():
+        raw_in[:, 5:8, :] = jnp.zeros((32, 3, 128), F32)
+
     sides = jnp.where(has_low, 1, 0) + jnp.where(has_high, 1, 0)
-    waits = sides + 8 - centre_i + 3 + 14 * centre_i
+    waits = sides + 8 - centre_i + 3 + 63 * centre_i
     waits = waits + jnp.where(imports, 1, 0) + centre_i * core
     pl.semaphore_wait(barrier, waits)
 
@@ -276,19 +275,19 @@
         def _():
             wait_for(halo_in.at[turn, 1], halo_recv.at[turn, 1])
 
+    raw_slot = raw_in.at[dom, pl.ds(0, 5)]
+    for n in range(8):
+        to_dom = (3 + n // 4) * 4 + n % 4
+
+        @pl.when(to_dom != dom)
+        def _():
+            remote(raw_out.at[n], raw_slot, raw_send, raw_recv, level, to_dom).start()
+
+        @pl.when(to_dom == dom)
+        def _():
+            pltpu.make_async_copy(raw_out.at[n], raw_slot, raw_recv).start()
+
     start_halo(0)
-
-    @pl.loop(0, 8)
-    def _(n):
-        to_dom = (3 + n // 4) * 4 + n % 4
-
-        @pl.when(to_dom != dom)
-        def _():
-            remote(raw_out.at[n], raw_in.at[dom], raw_send, raw_recv, level, to_dom).start()
-
-        @pl.when(to_dom == dom)
-        def _():
-            pltpu.make_async_copy(raw_out.at[n], raw_in.at[dom], raw_recv).start()
 
     @pl.when(centre & (core == 0))
     def _():
@@ -360,16 +359,15 @@
             fill_halo(turn + 1, fine_e, mid_e)
             start_halo(turn + 1)
 
-    sweep(0)
 
     @pl.when(centre)
     def _():
-        wait_for(raw_in, raw_recv)
+        wait_for(raw_in.at[:, pl.ds(0, 5)], raw_recv)
         rows = lax.broadcasted_iota(jnp.int32, (32, 8, 128), 1)
         cols = lax.broadcasted_iota(jnp.int32, (32, 8, 128), 2)
         value = raw_in[...]
         first = jnp.broadcast_to(value[:, 4:5, :], (32, 8, 128))
-        second = jnp.broadcast_to(value[:, 5:6, :], (32, 8, 128))
+        second = pltpu.roll(first, 64, 2)
         picks = jnp.where(rows < 2, first, second)
         wanted = (rows < 4) & (cols // 8 == rows % 2)
         picks = jnp.where(wanted, picks, 0.0).reshape(256, 128).astype(BF16)
@@ -389,7 +387,7 @@
             def _():
                 pltpu.make_async_copy(res_out, res_in.at[mine], res_recv).start()
 
-    sweep(1)
+    sweep(0)
 
     @pl.when(centre)
     def _():
@@ -411,52 +409,47 @@
             corr_out[peer, 1:2, :] = corr[8 + peer : 9 + peer, :]
         row = jnp.where(core == 0, half, 1 - half) * 4 + y_pos
 
-        @pl.loop(0, 8)
-        def _(peer):
+        slot = final.at[x_pos, z_two, row]
+
+        def result_to(peer, other_z):
+            return remote(
+                corr_out.at[peer],
+                slot,
+                z_send,
+                z_recv.at[z_two],
+                half * 8 + peer,
+                other_z * 4 + x_pos,
+            )
+
+        @pl.loop(0, 7)
+        def _(step):
+            other_z = (z_pos + 4 + step + jnp.where(step > 3, 1, 0)) % 8
+            for peer in range(8):
+                result_to(peer, other_z).start()
+
+        for peer in range(8):
+
             @pl.when(peer != mine)
             def _():
-                remote(
-                    corr_out.at[peer], corr_in.at[row], corr_send, corr_recv, half * 8 + peer, dom
-                ).start()
+                result_to(peer, z_pos).start()
 
             @pl.when(peer == mine)
             def _():
-                pltpu.make_async_copy(corr_out.at[peer], corr_in.at[row], corr_recv).start()
-
+                pltpu.make_async_copy(corr_out.at[peer], slot, z_recv.at[z_two]).start()
+
+    sweep(1)
     sweep(2)
-
-    @pl.when(centre)
-    def _():
-        wait_for(corr_in, corr_recv)
-
-        @pl.loop(0, 8)
-        def _(other_z):
-            @pl.when(other_z != z_pos)
-            def _():
-                remote(
-                    corr_in,
-                    final.at[x_pos, z_two],
-                    z_send,
-                    z_recv,
-                    level,
-                    other_z * 4 + x_pos,
-                ).start()
-
-            @pl.when(other_z == z_pos)
-            def _():
-                pltpu.make_async_copy(corr_in, final.at[x_pos, z_two], z_recv).start()
-
-    wait_for(final.at[0], z_recv)
-
-    for step in range(1, 4):
-        remote(
-            final.at[x_pos],
-            final.at[x_pos],
-            x_send,
-            x_recv,
-            level,
-            z_pos * 4 + (x_pos + step) % 4,
-        ).start()
+    for which in range(2):
+        wait_for(final.at[0, which], z_recv.at[which])
+        for step in range(1, 4):
+            remote(
+                final.at[x_pos, which],
+                final.at[x_pos, which],
+                x_send,
+                x_recv,
+                level,
+                z_pos * 4 + (x_pos + step) % 4,
+            ).start()
     wait_for(final.at[pl.ds(0, 3)], x_recv)
 
     for j in range(2):
@@ -491,8 +484,7 @@
     def _():
         wait_for(raw_out.at[pl.ds(0, 7)], raw_send)
         wait_for(res_in.at[pl.ds(0, 7)], res_send)
-        wait_for(corr_out.at[pl.ds(0, 7)], corr_send)
-        wait_for(raw_in.at[pl.ds(0, 14)], z_send)
+        wait_for(spare, z_send)
 
 
 def shards(
@@ -537,14 +529,14 @@
             vmem((4, 32, 128), BF16),
             vmem((3, 3, 16, 128), F32),
             vmem((3, 2, 3, 16, 128), F32),
-            vmem((8, 8, 128), F32),
+            vmem((8, 5, 128), F32),
             vmem((32, 8, 128), F32),
             vmem((16, 128), F32),
             vmem((8, 16, 128), F32),
             vmem((2, 64, 1024), F32),
             vmem((256, 1024), BF16),
             vmem((8, 2, 128), F32),
-            vmem((8, 2, 128), F32),
+            vmem((63, 2, 128), F32),
             vmem((4, 2, 8, 2, 128), F32),
             vmem((16, 128), F32),
             vmem((2, 16, 128), F32),
@@ -558,9 +550,7 @@
             dma,
             dma,
             dma,
-            dma,
-            dma,
-            dma,
+            dma((2,)),
             dma,
             dma,
         ],

time: 41.7 us -> 37.1 us (0.89)
  Pallas kernels: 39.4 us -> 34.7 us
    pallas_call x1, Pallas kernels: 39.4 us -> 34.7 us  [shards(): pl.pallas_call(kernel, out_shape=jax.ShapeDtypeStruct(right_side.shape, F...]
where the time goes in v3:
time: 37.1 us; the launch traced here: 36.7 us
  Pallas kernels  34.7 us (94%)
  local copies, waits for them, and re-layouts  1.38 us (4%)
  between operations  0.66 us (2%)
    pallas_call x1, Pallas kernels, shards(): pl.pallas_call(kernel, out_shape=jax.ShapeDtypeStruct(right_side.shape, F...  34.7 us
    unnamed x1, local copies, waits for them, and re-layouts  1.38 us

profile of v3, /device:TPU:1, one launch (start us, length us, event | category | flops | bytes accessed | tf_op | source)
XLA Modules:
  0.0 36.7 jit_solution(14787731918860221974)
XLA Ops:
  0.7 34.7 %shard_map.100 = f32[4,16,128]{2,1,0:T(8,128)} custom-call(s32[4,8]{1,0:T(4,128)} %fine_cols_hbm.1, s32[2]{0:T(128)} %fine_edges_hbm.1, s32[2,8]{1,0:T(2,128)} %mid_cols_hbm.1, s32[1]{0:T(128)S(6)} %copy.12.mid_edges_hbm, s32[4]{0:T(128)} %fine_map_hbm.1, s32[2]{0:T(128)} %mid_map_hbm.1, f32[4,16,128]{2,1,0:T(8,128)} %source_hbm.1, ...), custom_call_target="tpu_custom_call" | custom-call | tf_op jit(solution)/shard_map/pallas_call | solution.py:506
  35.3 1.4 %copy.13 = f32[4,16,128]{2,1,0:T(8,128)} copy(f32[4,16,128]{2,1,0:T(8,128)} %shard_map.100) | data formatting | bytes 65536

commit v4 on v3

--- a/solution.py
+++ b/solution.py
@@ -86,6 +86,7 @@
     final,
     picked,
     joined,
+    partial,
     load_sem,
     halo_send,
     halo_recv,
@@ -140,8 +141,7 @@
         )
     ]
     load_source = pltpu.make_async_copy(source_hbm, source, load_sem.at[0])
-    load_source.start()
-    for load in load_small:
+    for load in load_small[:2] + [load_source] + load_small[2:]:
         load.start()
     load_fine = [
         pltpu.make_async_copy(fine_hbm.at[r], fine_raw.at[r], load_sem.at[1 + r]) for r in range(4)
@@ -149,9 +149,6 @@
     load_mid = [
         pltpu.make_async_copy(mid_hbm.at[r], mid_raw.at[r], load_sem.at[5 + r]) for r in range(2)
     ]
-    for load in load_fine + load_mid:
-        load.start()
-
     barrier = pltpu.get_barrier_semaphore()
 
     def greet(to_level, to_dom):
@@ -192,6 +189,9 @@
             from_dom = jnp.where(z_pos == 3, 7, 0) * 4 + x_pos
             greet((1 - half) * 8 + y_pos * 2, from_dom)
             greet((1 - half) * 8 + y_pos * 2 + 1, from_dom)
+
+    for load in load_fine + load_mid:
+        load.start()
 
     for load in load_small:
         load.wait()
@@ -423,7 +423,8 @@
 
         @pl.loop(0, 7)
         def _(step):
-            other_z = (z_pos + 4 + step + jnp.where(step > 3, 1, 0)) % 8
+            other_z = jnp.where(step % 2 == 0, step // 2, 7 - step // 2)
+            other_z = jnp.where(other_z == z_pos, 7 - z_pos, other_z)
             for peer in range(8):
                 result_to(peer, other_z).start()
 
@@ -439,6 +440,9 @@
 
     sweep(1)
     sweep(2)
+    for i in range(4):
+        partial[i] = DAMPING * (fine_e[i] + MID_WEIGHT * mid_e[fine_map[i]])
+
     for which in range(2):
         wait_for(final.at[0, which], z_recv.at[which])
         for step in range(1, 4):
@@ -456,9 +460,9 @@
         for n in range(8):
             first = 4 * (n // 2) + 2 * (n % 2)
             picked[first : first + 2, :] = final[n // 2, n % 2, mid_map[j]]
-        joined[j] = mid_e[j] + (COARSE_WEIGHT * COARSE_WEIGHT) * picked[...]
+        joined[j] = (DAMPING * MID_WEIGHT * COARSE_WEIGHT * COARSE_WEIGHT) * picked[...]
     for i in range(4):
-        out[i] = DAMPING * (fine_e[i] + MID_WEIGHT * joined[fine_map[i]])
+        out[i] = partial[i] + joined[fine_map[i]]
 
     for turn in range(3):
 
@@ -540,6 +544,7 @@
             vmem((4, 2, 8, 2, 128), F32),
             vmem((16, 128), F32),
             vmem((2, 16, 128), F32),
+            vmem((4, 16, 128), F32),
             dma((13,)),
             dma((3, 2)),
             dma((3, 2)),
@@ -555,19 +560,24 @@
             dma,
         ],
         compiler_params=pltpu.CompilerParams(
-            collective_id=0, has_side_effects=True, vmem_limit_bytes=67043328
+            collective_id=0, has_side_effects=True, vmem_limit_bytes=40 * 1024 * 1024
         ),
     )(
-        fine_cols,
-        fine_edges,
-        mid_cols,
-        mid_edges,
-        fine_map,
-        mid_map,
-        right_side,
-        fine_blocks,
-        mid_blocks,
-        coarse_inverse,
+        *[
+            operand if operand is mid_edges else pltpu.with_memory_space_constraint(operand, pltpu.HBM)
+            for operand in (
+                fine_cols,
+                fine_edges,
+                mid_cols,
+                mid_edges,
+                fine_map,
+                mid_map,
+                right_side,
+                fine_blocks,
+                mid_blocks,
+                coarse_inverse,
+            )
+        ]
     )
 
 

time: 37.1 us -> 35.7 us (0.962)
  local copies, waits for them, and re-layouts: 1.38 us -> 0.62 us
  Pallas kernels: 34.7 us -> 34.1 us
    unnamed x1, local copies, waits for them, and re-layouts: 1.38 us -> 0.62 us
    pallas_call x1, Pallas kernels: 34.7 us -> 34.1 us  [shards(): pl.pallas_call(kernel, out_shape=jax.ShapeDtypeStruct(right_side.shape, F...]
where the time goes in v4:
time: 35.7 us; the launch traced here: 35.3 us
  Pallas kernels  34.1 us (96%)
  between operations  0.66 us (2%)
  local copies, waits for them, and re-layouts  0.62 us (2%)
    pallas_call x1, Pallas kernels, shards(): pl.pallas_call(kernel, out_shape=jax.ShapeDtypeStruct(right_side.shape, F...  34.1 us

profile of v4, /device:TPU:1, one launch (start us, length us, event | category | flops | bytes accessed | tf_op | source)
XLA Modules:
  0.0 35.3 jit_solution(8163683908083542986)
XLA Ops:
  0.7 34.1 %shard_map.100 = f32[4,16,128]{2,1,0:T(8,128)S(1)} custom-call(s32[4,8]{1,0:T(4,128)} %fine_cols_hbm.1, s32[2]{0:T(128)} %fine_edges_hbm.1, s32[2,8]{1,0:T(2,128)} %mid_cols_hbm.1, s32[1]{0:T(128)S(6)} %copy.12.mid_edges_hbm, s32[4]{0:T(128)} %fine_map_hbm.1, s32[2]{0:T(128)} %mid_map_hbm.1, f32[4,16,128]{2,1,0:T(8,128)} %source_hbm.1, ...), custom_call_target="tpu_custom_call" | custom-call | tf_op jit(solution)/shard_map/pallas_call | solution.py:510
  34.7 0.6 %copy.13 = f32[4,16,128]{2,1,0:T(8,128)} copy(f32[4,16,128]{2,1,0:T(8,128)S(1)} %shard_map.100) | data formatting | bytes 65536

commit v5 on v4

--- a/solution.py
+++ b/solution.py
@@ -127,6 +127,32 @@
             device_id_type=pl.DeviceIdType.MESH,
         )
 
+    barrier = pltpu.get_barrier_semaphore()
+
+    def greet(to_level, to_dom):
+        pl.semaphore_signal(
+            barrier, inc=1, device_id=(to_level, to_dom), device_id_type=pl.DeviceIdType.MESH
+        )
+
+    @pl.when(centre)
+    def _():
+        for other_z in (7, 0, 6, 1, 5, 2, 4, 3):
+            for other_x in range(4):
+
+                @pl.when((z_pos != other_z) | (x_pos != other_x))
+                def _():
+                    greet(level, other_z * 4 + other_x)
+
+        @pl.when(core == 0)
+        def _():
+            greet(level + 1, dom)
+
+        @pl.when(core == 1)
+        def _():
+            from_dom = jnp.where(z_pos == 3, 7, 0) * 4 + x_pos
+            greet((1 - half) * 8 + y_pos * 2, from_dom)
+            greet((1 - half) * 8 + y_pos * 2 + 1, from_dom)
+
     load_small = [
         pltpu.make_async_copy(src, dst, load_sem.at[7 + n])
         for n, (src, dst) in enumerate(
@@ -149,13 +175,6 @@
     load_mid = [
         pltpu.make_async_copy(mid_hbm.at[r], mid_raw.at[r], load_sem.at[5 + r]) for r in range(2)
     ]
-    barrier = pltpu.get_barrier_semaphore()
-
-    def greet(to_level, to_dom):
-        pl.semaphore_signal(
-            barrier, inc=1, device_id=(to_level, to_dom), device_id_type=pl.DeviceIdType.MESH
-        )
-
     @pl.when(has_low)
     def _():
         greet(level, dom - 1)
@@ -163,6 +182,9 @@
     @pl.when(has_high)
     def _():
         greet(level, dom + 1)
+
+    for step in range(1, 4):
+        greet(level, z_pos * 4 + (x_pos + step) % 4)
 
     for other_z in (3, 4):
         for peer in range(8):
@@ -170,25 +192,6 @@
             @pl.when((z_pos != other_z) | (mine != peer))
             def _():
                 greet(half * 8 + peer, other_z * 4 + x_pos)
-
-    for step in range(1, 4):
-        greet(level, z_pos * 4 + (x_pos + step) % 4)
-
-    @pl.when(centre)
-    def _():
-        @pl.loop(1, 32)
-        def _(step):
-            greet(level, (dom + step) % 32)
-
-        @pl.when(core == 0)
-        def _():
-            greet(level + 1, dom)
-
-        @pl.when(core == 1)
-        def _():
-            from_dom = jnp.where(z_pos == 3, 7, 0) * 4 + x_pos
-            greet((1 - half) * 8 + y_pos * 2, from_dom)
-            greet((1 - half) * 8 + y_pos * 2 + 1, from_dom)
 
     for load in load_fine + load_mid:
         load.start()
@@ -359,6 +362,7 @@
             fill_halo(turn + 1, fine_e, mid_e)
             start_halo(turn + 1)
 
+    sweep(0)
 
     @pl.when(centre)
     def _():
@@ -387,7 +391,6 @@
             def _():
                 pltpu.make_async_copy(res_out, res_in.at[mine], res_recv).start()
 
-    sweep(0)
 
     @pl.when(centre)
     def _():
@@ -439,10 +442,6 @@
                 pltpu.make_async_copy(corr_out.at[peer], slot, z_recv.at[z_two]).start()
 
     sweep(1)
-    sweep(2)
-    for i in range(4):
-        partial[i] = DAMPING * (fine_e[i] + MID_WEIGHT * mid_e[fine_map[i]])
-
     for which in range(2):
         wait_for(final.at[0, which], z_recv.at[which])
         for step in range(1, 4):
@@ -454,6 +453,10 @@
                 level,
                 z_pos * 4 + (x_pos + step) % 4,
             ).start()
+    sweep(2)
+    for i in range(4):
+        partial[i] = DAMPING * (fine_e[i] + MID_WEIGHT * mid_e[fine_map[i]])
+
     wait_for(final.at[pl.ds(0, 3)], x_recv)
 
     for j in range(2):

time: 35.7 us -> 34.9 us (0.978)
  Pallas kernels: 34.1 us -> 33.5 us
    pallas_call x1, Pallas kernels: 34.1 us -> 33.5 us  [shards(): pl.pallas_call(kernel, out_shape=jax.ShapeDtypeStruct(right_side.shape, F...]
where the time goes in v5:
time: 34.9 us; the launch traced here: 34.8 us
  Pallas kernels  33.5 us (96%)
  between operations  0.66 us (2%)
  local copies, waits for them, and re-layouts  0.62 us (2%)
    pallas_call x1, Pallas kernels, shards(): pl.pallas_call(kernel, out_shape=jax.ShapeDtypeStruct(right_side.shape, F...  33.5 us

profile of v5, /device:TPU:1, one launch (start us, length us, event | category | flops | bytes accessed | tf_op | source)
XLA Modules:
  0.0 34.8 jit_solution(17315691604668259000)
XLA Ops:
  0.7 33.5 %shard_map.100 = f32[4,16,128]{2,1,0:T(8,128)S(1)} custom-call(s32[4,8]{1,0:T(4,128)} %fine_cols_hbm.1, s32[2]{0:T(128)} %fine_edges_hbm.1, s32[2,8]{1,0:T(2,128)} %mid_cols_hbm.1, s32[1]{0:T(128)S(6)} %copy.12.mid_edges_hbm, s32[4]{0:T(128)} %fine_map_hbm.1, s32[2]{0:T(128)} %mid_map_hbm.1, f32[4,16,128]{2,1,0:T(8,128)} %source_hbm.1, ...), custom_call_target="tpu_custom_call" | custom-call | tf_op jit(solution)/shard_map/pallas_call | solution.py:513
  34.2 0.6 %copy.13 = f32[4,16,128]{2,1,0:T(8,128)} copy(f32[4,16,128]{2,1,0:T(8,128)S(1)} %shard_map.100) | data formatting | bytes 65536

commit v6 on v5

--- a/solution.py
+++ b/solution.py
@@ -97,6 +97,7 @@
     res_send,
     res_recv,
     z_send,
+    early_send,
     z_recv,
     x_send,
     x_recv,
@@ -114,6 +115,7 @@
     z_two = jnp.where(z_pos == 4, 1, 0)
     has_low = dom > 0
     has_high = dom < 31
+    early = (half == 0) & (z_pos == 0)
     import_z = jnp.where(z_pos == 7, 3, 4)
     imports = (z_pos == 0) | (z_pos == 7)
 
@@ -183,8 +185,10 @@
     def _():
         greet(level, dom + 1)
 
-    for step in range(1, 4):
-        greet(level, z_pos * 4 + (x_pos + step) % 4)
+    @pl.when(jnp.logical_not(early))
+    def _():
+        for step in range(1, 4):
+            greet(level, z_pos * 4 + (x_pos + step) % 4)
 
     for other_z in (3, 4):
         for peer in range(8):
@@ -192,6 +196,13 @@
             @pl.when((z_pos != other_z) | (mine != peer))
             def _():
                 greet(half * 8 + peer, other_z * 4 + x_pos)
+
+    @pl.when(early)
+    def _():
+        for step in range(1, 4):
+            for other_z in (3, 4):
+                for peer in range(8):
+                    greet(peer, other_z * 4 + (x_pos + step) % 4)
 
     for load in load_fine + load_mid:
         load.start()
@@ -237,6 +248,7 @@
 
     sides = jnp.where(has_low, 1, 0) + jnp.where(has_high, 1, 0)
     waits = sides + 8 - centre_i + 3 + 63 * centre_i
+    waits = waits + jnp.where(centre & (half == 0), 24, 0) - jnp.where(early, 3, 0)
     waits = waits + jnp.where(imports, 1, 0) + centre_i * core
     pl.semaphore_wait(barrier, waits)
 
@@ -424,12 +436,25 @@
                 other_z * 4 + x_pos,
             )
 
-        @pl.loop(0, 7)
-        def _(step):
-            other_z = jnp.where(step % 2 == 0, step // 2, 7 - step // 2)
-            other_z = jnp.where(other_z == z_pos, 7 - z_pos, other_z)
+        @pl.when(half == 0)
+        def _():
+            @pl.loop(1, 4)
+            def _(step):
+                for peer in range(8):
+                    remote(
+                        corr_out.at[peer],
+                        slot,
+                        early_send,
+                        z_recv.at[z_two],
+                        peer,
+                        (x_pos + step) % 4,
+                    ).start()
+
+        for first_half, second_half in ((0, 7), (1, 0), (2, 6), (7, 1), (6, 5), (5, 2)):
             for peer in range(8):
-                result_to(peer, other_z).start()
+                result_to(peer, jnp.where(half == 0, first_half, second_half)).start()
+        for peer in range(8):
+            result_to(peer, 7 - z_pos).start()
 
         for peer in range(8):
 
@@ -442,22 +467,32 @@
                 pltpu.make_async_copy(corr_out.at[peer], slot, z_recv.at[z_two]).start()
 
     sweep(1)
-    for which in range(2):
-        wait_for(final.at[0, which], z_recv.at[which])
-        for step in range(1, 4):
-            remote(
-                final.at[x_pos, which],
-                final.at[x_pos, which],
-                x_send,
-                x_recv,
-                level,
-                z_pos * 4 + (x_pos + step) % 4,
-            ).start()
+    @pl.when(jnp.logical_not(early))
+    def _():
+        for which in range(2):
+            wait_for(final.at[0, which], z_recv.at[which])
+            for step in range(1, 4):
+                remote(
+                    final.at[x_pos, which],
+                    final.at[x_pos, which],
+                    x_send,
+                    x_recv,
+                    level,
+                    z_pos * 4 + (x_pos + step) % 4,
+                ).start()
+
     sweep(2)
     for i in range(4):
         partial[i] = DAMPING * (fine_e[i] + MID_WEIGHT * mid_e[fine_map[i]])
 
-    wait_for(final.at[pl.ds(0, 3)], x_recv)
+    @pl.when(early)
+    def _():
+        for which in range(2):
+            wait_for(final.at[pl.ds(0, 2)], z_recv.at[which])
+
+    @pl.when(jnp.logical_not(early))
+    def _():
+        wait_for(final.at[pl.ds(0, 3)], x_recv)
 
     for j in range(2):
         for n in range(8):
@@ -477,7 +512,9 @@
         def _():
             wait_for(halo_out.at[turn], halo_send.at[turn, 1])
 
-    wait_for(final.at[pl.ds(0, 3)], x_send)
+    @pl.when(jnp.logical_not(early))
+    def _():
+        wait_for(final.at[pl.ds(0, 3)], x_send)
 
     @pl.when(imports | (centre & (core == 1)))
     def _():
@@ -492,6 +529,10 @@
         wait_for(raw_out.at[pl.ds(0, 7)], raw_send)
         wait_for(res_in.at[pl.ds(0, 7)], res_send)
         wait_for(spare, z_send)
+
+        @pl.when(half == 0)
+        def _():
+            wait_for(spare.at[pl.ds(0, 24)], early_send)
 
 
 def shards(
@@ -558,6 +599,7 @@
             dma,
             dma,
             dma,
+            dma,
             dma((2,)),
             dma,
             dma,

time: 34.9 us -> 34.2 us (0.980)
  Pallas kernels: 33.5 us -> 32.5 us
    pallas_call x1, Pallas kernels: 33.5 us -> 32.5 us  [shards(): pl.pallas_call(kernel, out_shape=jax.ShapeDtypeStruct(right_side.shape, F...]
where the time goes in v6:
time: 34.2 us; the launch traced here: 33.8 us
  Pallas kernels  32.5 us (95%)
  between operations  0.66 us (2%)
  local copies, waits for them, and re-layouts  0.62 us (2%)
    pallas_call x1, Pallas kernels, shards(): pl.pallas_call(kernel, out_shape=jax.ShapeDtypeStruct(right_side.shape, F...  32.5 us

profile of v6, /device:TPU:1, one launch (start us, length us, event | category | flops | bytes accessed | tf_op | source)
XLA Modules:
  0.0 33.8 jit_solution(14454125049811112423)
XLA Ops:
  0.7 32.5 %shard_map.100 = f32[4,16,128]{2,1,0:T(8,128)S(1)} custom-call(s32[4,8]{1,0:T(4,128)} %fine_cols_hbm.1, s32[2]{0:T(128)} %fine_edges_hbm.1, s32[2,8]{1,0:T(2,128)} %mid_cols_hbm.1, s32[1]{0:T(128)S(6)} %copy.12.mid_edges_hbm, s32[4]{0:T(128)} %fine_map_hbm.1, s32[2]{0:T(128)} %mid_map_hbm.1, f32[4,16,128]{2,1,0:T(8,128)} %source_hbm.1, ...), custom_call_target="tpu_custom_call" | custom-call | tf_op jit(solution)/shard_map/pallas_call | solution.py:554
  33.2 0.6 %copy.13 = f32[4,16,128]{2,1,0:T(8,128)} copy(f32[4,16,128]{2,1,0:T(8,128)S(1)} %shard_map.100) | data formatting | bytes 65536

commit v7 on v6

--- a/solution.py
+++ b/solution.py
@@ -291,16 +291,23 @@
             wait_for(halo_in.at[turn, 1], halo_recv.at[turn, 1])
 
     raw_slot = raw_in.at[dom, pl.ds(0, 5)]
-    for n in range(8):
-        to_dom = (3 + n // 4) * 4 + n % 4
-
-        @pl.when(to_dom != dom)
-        def _():
-            remote(raw_out.at[n], raw_slot, raw_send, raw_recv, level, to_dom).start()
-
-        @pl.when(to_dom == dom)
-        def _():
-            pltpu.make_async_copy(raw_out.at[n], raw_slot, raw_recv).start()
+    far = jnp.where(z_pos < 4, 1, 0)
+    for step, near in ((2, 0), (1, 0), (3, 0), (2, 1), (0, 0), (1, 1), (3, 1)):
+        which = jnp.where(near == 1, 1 - far, far)
+        to_x = (x_pos + step) % 4
+        to_dom = (3 + which) * 4 + to_x
+        remote(
+            raw_out.at[which * 4 + to_x], raw_slot, raw_send, raw_recv, level, to_dom
+        ).start()
+    last = raw_out.at[(1 - far) * 4 + x_pos]
+
+    @pl.when(jnp.logical_not(centre))
+    def _():
+        remote(last, raw_slot, raw_send, raw_recv, level, (4 - far) * 4 + x_pos).start()
+
+    @pl.when(centre)
+    def _():
+        pltpu.make_async_copy(last, raw_slot, raw_recv).start()
 
     start_halo(0)
 
@@ -393,15 +400,10 @@
         total = full[:16, :128] + full[:16, 128:]
         res_out[...] = total
 
-        @pl.loop(0, 8)
-        def _(peer):
-            @pl.when(peer != mine)
-            def _():
-                remote(res_out, res_in.at[mine], res_send, res_recv, half * 8 + peer, dom).start()
-
-            @pl.when(peer == mine)
-            def _():
-                pltpu.make_async_copy(res_out, res_in.at[mine], res_recv).start()
+        for step in (4, 3, 5, 2, 6, 1, 7):
+            to_level = half * 8 + (mine + step) % 8
+            remote(res_out, res_in.at[mine], res_send, res_recv, to_level, dom).start()
+        pltpu.make_async_copy(res_out, res_in.at[mine], res_recv).start()
 
 
     @pl.when(centre)
@@ -436,11 +438,12 @@
                 other_z * 4 + x_pos,
             )
 
+        peers = [(mine + step) % 8 for step in (4, 5, 3, 2, 6, 1, 7, 0)]
+
         @pl.when(half == 0)
         def _():
-            @pl.loop(1, 4)
-            def _(step):
-                for peer in range(8):
+            for peer in peers:
+                for step in (2, 1, 3, 0):
                     remote(
                         corr_out.at[peer],
                         slot,
@@ -450,28 +453,26 @@
                         (x_pos + step) % 4,
                     ).start()
 
-        for first_half, second_half in ((0, 7), (1, 0), (2, 6), (7, 1), (6, 5), (5, 2)):
-            for peer in range(8):
+        @pl.when(half == 1)
+        def _():
+            for peer in peers:
+                result_to(peer, 7).start()
+
+        for first_half, second_half in ((1, 0), (2, 6), (7, 1), (6, 5), (5, 2)):
+            for peer in peers:
                 result_to(peer, jnp.where(half == 0, first_half, second_half)).start()
-        for peer in range(8):
+        for peer in peers:
             result_to(peer, 7 - z_pos).start()
-
-        for peer in range(8):
-
-            @pl.when(peer != mine)
-            def _():
-                result_to(peer, z_pos).start()
-
-            @pl.when(peer == mine)
-            def _():
-                pltpu.make_async_copy(corr_out.at[peer], slot, z_recv.at[z_two]).start()
+        for peer in peers[:7]:
+            result_to(peer, z_pos).start()
+        pltpu.make_async_copy(corr_out.at[mine], slot, z_recv.at[z_two]).start()
 
     sweep(1)
     @pl.when(jnp.logical_not(early))
     def _():
         for which in range(2):
             wait_for(final.at[0, which], z_recv.at[which])
-            for step in range(1, 4):
+            for step in (2, 1, 3):
                 remote(
                     final.at[x_pos, which],
                     final.at[x_pos, which],
@@ -528,11 +529,14 @@
     def _():
         wait_for(raw_out.at[pl.ds(0, 7)], raw_send)
         wait_for(res_in.at[pl.ds(0, 7)], res_send)
-        wait_for(spare, z_send)
-
         @pl.when(half == 0)
         def _():
-            wait_for(spare.at[pl.ds(0, 24)], early_send)
+            wait_for(spare.at[pl.ds(0, 32)], early_send)
+            wait_for(spare.at[pl.ds(0, 55)], z_send)
+
+        @pl.when(half == 1)
+        def _():
+            wait_for(spare, z_send)
 
 
 def shards(

time: 34.2 us -> 34.1 us (level)
  the two profiles are of different devices: /device:TPU:1 before, /device:TPU:32 now
where the time goes in v7:
time: 34.1 us; the launch traced here: 33.9 us
  Pallas kernels  32.7 us (96%)
  between operations  0.66 us (2%)
  local copies, waits for them, and re-layouts  0.62 us (2%)
    pallas_call x1, Pallas kernels, shards(): pl.pallas_call(kernel, out_shape=jax.ShapeDtypeStruct(right_side.shape, F...  32.7 us

profile of v7, /device:TPU:32, one launch (start us, length us, event | category | flops | bytes accessed | tf_op | source)
XLA Modules:
  0.0 33.9 jit_solution(16902129756587888421)
XLA Ops:
  0.7 32.7 %shard_map.100 = f32[4,16,128]{2,1,0:T(8,128)S(1)} custom-call(s32[4,8]{1,0:T(4,128)} %fine_cols_hbm.1, s32[2]{0:T(128)} %fine_edges_hbm.1, s32[2,8]{1,0:T(2,128)} %mid_cols_hbm.1, s32[1]{0:T(128)S(6)} %copy.12.mid_edges_hbm, s32[4]{0:T(128)} %fine_map_hbm.1, s32[2]{0:T(128)} %mid_map_hbm.1, f32[4,16,128]{2,1,0:T(8,128)} %source_hbm.1, ...), custom_call_target="tpu_custom_call" | custom-call | tf_op jit(solution)/shard_map/pallas_call | solution.py:558
  33.3 0.6 %copy.13 = f32[4,16,128]{2,1,0:T(8,128)} copy(f32[4,16,128]{2,1,0:T(8,128)S(1)} %shard_map.100) | data formatting | bytes 65536

commit v8 on v7

--- a/solution.py
+++ b/solution.py
@@ -440,6 +440,9 @@
 
         peers = [(mine + step) % 8 for step in (4, 5, 3, 2, 6, 1, 7, 0)]
 
+        for peer in peers:
+            result_to(peer, jnp.where(half == 0, 1, 7)).start()
+
         @pl.when(half == 0)
         def _():
             for peer in peers:
@@ -456,9 +459,9 @@
         @pl.when(half == 1)
         def _():
             for peer in peers:
-                result_to(peer, 7).start()
-
-        for first_half, second_half in ((1, 0), (2, 6), (7, 1), (6, 5), (5, 2)):
+                result_to(peer, 0).start()
+
+        for first_half, second_half in ((2, 6), (7, 1), (6, 5), (5, 2)):
             for peer in peers:
                 result_to(peer, jnp.where(half == 0, first_half, second_half)).start()
         for peer in peers:

time: 34.1 us -> 33.5 us (0.982)
  the two profiles are of different devices: /device:TPU:32 before, /device:TPU:1 now
where the time goes in v8:
time: 33.5 us; the launch traced here: 33.3 us
  Pallas kernels  32 us (96%)
  between operations  0.66 us (2%)
  local copies, waits for them, and re-layouts  0.62 us (2%)
    pallas_call x1, Pallas kernels, shards(): pl.pallas_call(kernel, out_shape=jax.ShapeDtypeStruct(right_side.shape, F...  32 us

profile of v8, /device:TPU:1, one launch (start us, length us, event | category | flops | bytes accessed | tf_op | source)
XLA Modules:
  0.0 33.3 jit_solution(8784740320459459040)
XLA Ops:
  0.7 32.0 %shard_map.100 = f32[4,16,128]{2,1,0:T(8,128)S(1)} custom-call(s32[4,8]{1,0:T(4,128)} %fine_cols_hbm.1, s32[2]{0:T(128)} %fine_edges_hbm.1, s32[2,8]{1,0:T(2,128)} %mid_cols_hbm.1, s32[1]{0:T(128)S(6)} %copy.12.mid_edges_hbm, s32[4]{0:T(128)} %fine_map_hbm.1, s32[2]{0:T(128)} %mid_map_hbm.1, f32[4,16,128]{2,1,0:T(8,128)} %source_hbm.1, ...), custom_call_target="tpu_custom_call" | custom-call | tf_op jit(solution)/shard_map/pallas_call | solution.py:561
  32.7 0.6 %copy.13 = f32[4,16,128]{2,1,0:T(8,128)} copy(f32[4,16,128]{2,1,0:T(8,128)S(1)} %shard_map.100) | data formatting | bytes 65536
